TPU v7x, 512 devices: a whole 4x8x8 slice. The times are simulated.
512 devices in a mesh: shard: 64 (over x, z, core), tensor: 8 (over y).
Axes of the slice: x: 4, y: 8, z: 8, core: 2. Of those that a mesh axis runs over, the one named last changes fastest.
Arguments:
- grad: float32 [8, 512, 1024], P(None, 'shard', 'tensor'), may hold values from -500 to 500
- momentum: float32 [8, 512, 1024], P(None, 'shard', 'tensor'), may hold values from -6 to 6
- weight: float32 [8, 512, 1024], P(None, 'shard', 'tensor'), may hold values from -0.625 to 0.625
Outputs:
- new_weight: float32 [8, 512, 1024], P(None, 'shard', 'tensor')
- new_momentum: float32 [8, 512, 1024], P(None, 'shard', 'tensor')
- update: float32 [8, 512, 1024], P(None, 'shard', 'tensor')
All inputs are finite; a program needn't handle non-finite values.
Results may differ from a plain program's by a relative error of at most 0.0078.
Values may be sent and summed in bfloat16 or wider, within the bound.
A program may use at most 64 MiB of HBM per device.

v0:
```python
import math
import jax
import jax.numpy as jnp
from jax import lax
from jax.sharding import PartitionSpec as P

ITERS = 3
mu_decay = 0.95
learn_rate = 0.05
weight_decay = 0.1
update_gain = 0.2
first_coef = 3.4445
second_coef = -4.775
third_coef = 2.0315
epsilon = 1e-07


def polish(iterate, gram):
    wide = iterate.astype(jnp.float32)
    squared = jnp.dot(gram, gram, precision=lax.Precision.HIGHEST)
    poly = second_coef * gram + third_coef * squared
    mixed = jnp.dot(poly, wide, precision=lax.Precision.HIGHEST)
    fresh = first_coef * wide + mixed
    return fresh.astype(jnp.bfloat16)


def on_device(grad, momentum, weight):
    mats, rows_local, cols_local = grad.shape
    n_tensor = lax.axis_size("tensor")
    new_momentum = mu_decay * momentum + grad
    advance = (grad + mu_decay * new_momentum).astype(jnp.bfloat16)
    mine = lax.all_to_all(advance, "tensor", split_axis=0, concat_axis=2, tiled=True)
    whole = lax.all_gather(mine, "shard", axis=1, tiled=True)[0]
    wide = whole.astype(jnp.float32)
    frob = jnp.sqrt(jnp.sum(wide * wide)) + epsilon
    iterate = (wide / frob).astype(jnp.bfloat16)
    for step in range(ITERS):
        gram = jnp.dot(iterate, iterate.T, preferred_element_type=jnp.float32)
        iterate = polish(iterate, gram)
    start = lax.axis_index("shard") * rows_local
    rows = lax.dynamic_slice_in_dim(iterate, start, rows_local, axis=0)
    ortho = lax.all_to_all(rows[None], "tensor", split_axis=2, concat_axis=0, tiled=True)
    width = cols_local * n_tensor
    update = update_gain * math.sqrt(width) * ortho.astype(jnp.float32)
    new_weight = weight - learn_rate * (update + weight_decay * weight)
    return (new_weight, new_momentum, update)


def solution(mesh):
    in_specs = (P(None, "shard", "tensor"), P(None, "shard", "tensor"), P(None, "shard", "tensor"))
    out_specs = (P(None, "shard", "tensor"), P(None, "shard", "tensor"), P(None, "shard", "tensor"))
    return jax.shard_map(
        on_device, mesh=mesh, in_specs=in_specs, out_specs=out_specs, check_vma=False
    )
```

profile of v0, /device:TPU:1, one launch (start us, length us, event | category | flops | bytes accessed | tf_op | source)
XLA Modules:
  0.0 151.1 jit_solution(5558221943511022706)
XLA Ops:
  7.2 0.0 all-gather.2.cloned.1.call-start
  7.2 1.4 add_convert_fusion.2
  8.6 14.2 %all_to_all.27 = bf16[8,8,128]{2,1,0:T(8,128)(2,1)} all-to-all(bf16[8,8,128]{2,1,0:T(8,128)(2,1)S(1)} %get-tuple-element.3), channel_id=1, replica_groups=mesh['shard'=64,'tensor'=8] {'tensor'}, dimensions={0} | all-to-all | bytes 32768 | tf_op jit(solution)/shard_map/all_to_all | solution.py:32
  22.8 0.0 all-gather.2.cloned.1.call-update
  22.8 84.4 %all-gather.2.cloned.1.call-done = bf16[1,512,1024]{2,1,0:T(8,128)(2,1)} async-done(((bf16[1,8,1024]{2,1,0:T(8,128)(2,1)}), bf16[1,512,1024]{2,1,0:T(8,128)(2,1)}) %all-gather.2.cloned.1.call-update) | async-done | bytes 1048592 | tf_op jit(solution)/shard_map/all_gather | solution.py:33
  107.2 2.4 %fusion = f32[]{:T(128)} fusion(bf16[1,512,1024]{2,1,0:T(8,128)(2,1)} %all-gather.2.cloned.1.call-done), kind=kLoop, calls=%fused_computation.2 | loop fusion | flops 1572863 | bytes 1048580 | tf_op jit(solution)/shard_map/reduce_sum | solution.py:35
  110.2 2.3 %fusion.8 = f32[512,512]{1,0:T(8,128)S(1)} fusion(bf16[1,512,1024]{2,1,0:T(8,128)(2,1)} %all-gather.2.cloned.1.call-done, f32[]{:T(128)S(6)} %add.35), kind=kOutput, calls=%fused_computation.20 | convolution fusion | flops 538443776 | bytes 2097156 | tf_op jit(solution)/shard_map/dot_general | solution.py:38
  112.5 0.0 copy-start
  112.5 1.9 %fusion.4 = f32[512,512]{1,0:T(8,128)S(1)} fusion(f32[512,512]{1,0:T(8,128)S(1)} %fusion.8), kind=kOutput, calls=%fused_computation.11 | convolution fusion | flops 1611399168 | bytes 2097152 | tf_op jit(solution)/shard_map/dot_general | solution.py:20
  114.5 0.0 copy-done
  114.5 1.9 %add_convert_fusion.1 = bf16[512,1024]{1,0:T(8,128)(2,1)S(1)} fusion(f32[512,512]{1,0:T(8,128)S(1)} %fusion.4, f32[]{:T(128)S(6)} %add.35, bf16[1,512,1024]{2,1,0:T(8,128)(2,1)S(1)} %copy-done), kind=kOutput, calls=%fused_computation.5 | convolution fusion | flops 3226468352 | bytes 3145732 | tf_op jit(solution)/shard_map/dot_general | solution.py:22
  116.4 0.7 fusion.11
  117.1 1.9 %fusion.3 = f32[512,512]{1,0:T(8,128)S(1)} fusion(f32[512,512]{1,0:T(8,128)S(1)} %fusion.11), kind=kOutput, calls=%fused_computation.9 | convolution fusion | flops 1611399168 | bytes 2097152 | tf_op jit(solution)/shard_map/dot_general | solution.py:20
  119.1 1.9 %add_convert_fusion = bf16[512,1024]{1,0:T(8,128)(2,1)S(1)} fusion(bf16[512,1024]{1,0:T(8,128)(2,1)S(1)} %add_convert_fusion.1, f32[512,512]{1,0:T(8,128)S(1)} %fusion.3), kind=kOutput, calls=%fused_computation.4 | convolution fusion | flops 3223322624 | bytes 3145728 | tf_op jit(solution)/shard_map/dot_general | solution.py:22
  120.9 0.7 fusion.12
  121.7 1.9 %fusion.2 = f32[512,512]{1,0:T(8,128)S(1)} fusion(f32[512,512]{1,0:T(8,128)S(1)} %fusion.12), kind=kOutput, calls=%fused_computation.7 | convolution fusion | flops 1611399168 | bytes 2097152 | tf_op jit(solution)/shard_map/dot_general | solution.py:20
  123.6 2.0 %fusion.13 = f32[512,1024]{1,0:T(8,128)S(1)} fusion(f32[512,512]{1,0:T(8,128)S(1)} %fusion.2, bf16[512,1024]{1,0:T(8,128)(2,1)S(1)} %add_convert_fusion), kind=kOutput, calls=%fused_computation.23 | convolution fusion | flops 3221225472 | bytes 4194304 | tf_op jit(solution)/shard_map/dot_general | solution.py:22
  125.6 0.0 copy-start.2
  125.7 0.4 copy.7
  126.1 0.5 broadcast.39
  126.6 2.3 %reduce.1 = bf16[1024,8]{1,0:T(8,128)(2,1)S(1)} reduce(bf16[1024,1,8]{2,1,0:T(2,128)(2,1)S(1)} %bitcast.37, bf16[]{:T(256)} %broadcast.39), dimensions={1}, to_apply=%bitcast.18.reduce_sub_computation | reduce | bytes 32770
  128.8 0.3 reshape.19
  129.1 12.9 %all_to_all.28 = bf16[8,2,512]{2,1,0:T(2,128)(2,1)S(1)} all-to-all(bf16[8,2,512]{2,1,0:T(2,128)(2,1)S(1)} %reshape.19), channel_id=1, replica_groups=mesh['shard'=64,'tensor'=8] {'tensor'}, dimensions={0} | all-to-all | bytes 32768 | tf_op jit(solution)/shard_map/all_to_all | solution.py:42
  142.0 0.7 reshape.20
  142.7 0.7 convert_multiply_fusion.1
  143.4 0.2 copy.8
  143.6 0.0 copy-done.2
  143.6 0.0 copy-start.1
  143.6 0.6 multiply_subtract_fusion
  144.2 0.0 copy-done.1
  (1 shorter events, 0.0 us)
Async XLA Ops:
  7.2 100.0 %all-gather.2.cloned.1.call-start = ((), (), s32[]{:S(2)}) async-start(), calls=%async_computation.2 | async-start | bytes 1064960 | tf_op jit(solution)/shard_map/all_gather | solution.py:33
  112.5 1.9 %copy-start = (bf16[1,512,1024]{2,1,0:T(8,128)(2,1)S(1)}, bf16[1,512,1024]{2,1,0:T(8,128)(2,1)}, u32[]{:S(2)}) copy-start(bf16[1,512,1024]{2,1,0:T(8,128)(2,1)} %all-gather.2.cloned.1.call-done) | copy-start | bytes 3145732
  125.6 18.0 %copy-start.2 = (f32[8,8,128]{2,1,0:T(8,128)S(1)}, f32[8,8,128]{2,1,0:T(8,128)}, u32[]{:S(2)}) copy-start(f32[8,8,128]{2,1,0:T(8,128)} %param.5) | copy-start | bytes 98308
  143.6 0.6 copy-start.1
Sparse Core Ops, SparseCore 0:
  22.9 84.2 all-gather.1
where the time goes:
time: 151 us
  waiting for transfers between devices  84.4 us (56%)
  blocking collectives  27 us (18%)
  matrix products  15.3 us (10%)
  between operations  14.9 us (10%)
  other arithmetic  7.41 us (5%)
  local copies, waits for them, and re-layouts  2.04 us (1%)
    all_gather x1, waiting for transfers between devices, on_device(): whole = lax.all_gather(mine, 'shard', axis=1, tiled=True)[0]  84.4 us
    all_to_all x1, blocking collectives, on_device(): lax.all_to_all(advance, 'tensor', split_axis=0, concat_axis=2, tiled=True)  14.2 us
    all_to_all x1, blocking collectives, on_device(): lax.all_to_all(rows[None], 'tensor', split_axis=2, concat_axis=0, tiled=T...  12.9 us
    dot_general x3, matrix products, polish(): mixed = jnp.dot(poly, wide, precision=lax.Precision.HIGHEST)  5.81 us
    dot_general x3, matrix products, polish(): squared = jnp.dot(gram, gram, precision=lax.Precision.HIGHEST)  5.73 us
    dot_general x3, matrix products, on_device(): gram = jnp.dot(iterate, iterate.T, preferred_element_type=jnp.float32)  3.78 us
  transfers between devices with their start and end apart: 1, of which 1 were waited for; matrix products, arithmetic and copies ran while one was open for 0% of the time, Pallas kernels for 0%

commit v1 on v0

--- a/solution.py
+++ b/solution.py
@@ -29,7 +29,12 @@
     n_tensor = lax.axis_size("tensor")
     new_momentum = mu_decay * momentum + grad
     advance = (grad + mu_decay * new_momentum).astype(jnp.bfloat16)
-    mine = lax.all_to_all(advance, "tensor", split_axis=0, concat_axis=2, tiled=True)
+    mine = jnp.concatenate(
+        lax.all_to_all(
+            jnp.stack(jnp.split(advance, lax.axis_size("tensor"), axis=0)), "tensor", 0, 0
+        ),
+        axis=2,
+    )
     whole = lax.all_gather(mine, "shard", axis=1, tiled=True)[0]
     wide = whole.astype(jnp.float32)
     frob = jnp.sqrt(jnp.sum(wide * wide)) + epsilon

time: 151 us -> 151 us (level)
  no operation moved by 1% of the time
where the time goes in v1:
time: 151 us
  waiting for transfers between devices  84.4 us (56%)
  blocking collectives  27 us (18%)
  matrix products  15.3 us (10%)
  between operations  14.9 us (10%)
  other arithmetic  7.41 us (5%)
  local copies, waits for them, and re-layouts  2.09 us (1%)
    all_gather x1, waiting for transfers between devices, on_device(): whole = lax.all_gather(mine, 'shard', axis=1, tiled=True)[0]  84.4 us
    all_to_all x1, blocking collectives, on_device(): lax.all_to_all(jnp.stack(jnp.split(advance, lax.axis_size('tensor'), axis...  14.2 us
    all_to_all x1, blocking collectives, on_device(): lax.all_to_all(rows[None], 'tensor', split_axis=2, concat_axis=0, tiled=T...  12.9 us
    dot_general x3, matrix products, polish(): mixed = jnp.dot(poly, wide, precision=lax.Precision.HIGHEST)  5.81 us
    dot_general x3, matrix products, polish(): squared = jnp.dot(gram, gram, precision=lax.Precision.HIGHEST)  5.73 us
    dot_general x3, matrix products, on_device(): gram = jnp.dot(iterate, iterate.T, preferred_element_type=jnp.float32)  3.78 us
  transfers between devices with their start and end apart: 1, of which 1 were waited for; matrix products, arithmetic and copies ran while one was open for 0% of the time, Pallas kernels for 0%

profile of v1, /device:TPU:1, one launch (start us, length us, event | category | flops | bytes accessed | tf_op | source)
XLA Modules:
  0.0 151.2 jit_solution(14741303369283499735)
XLA Ops:
  7.2 0.0 all-gather.2.cloned.1.call-start
  7.2 1.4 add_convert_fusion.2
  8.7 14.2 %all_to_all.14 = bf16[8,1,8,128]{3,2,1,0:T(8,128)(2,1)} all-to-all(bf16[8,1,8,128]{3,2,1,0:T(8,128)(2,1)S(1)} %constant_dynamic-update-slice_fusion), channel_id=1, replica_groups=mesh['shard'=64,'tensor'=8] {'tensor'}, dimensions={0} | all-to-all | bytes 32768 | tf_op jit(solution)/shard_map/all_to_all | solution.py:33
  22.8 0.0 all-gather.2.cloned.1.call-update
  22.9 84.4 %all-gather.2.cloned.1.call-done = bf16[1,512,1024]{2,1,0:T(8,128)(2,1)} async-done(((bf16[1,8,1024]{2,1,0:T(8,128)(2,1)}), bf16[1,512,1024]{2,1,0:T(8,128)(2,1)}) %all-gather.2.cloned.1.call-update) | async-done | bytes 1048592 | tf_op jit(solution)/shard_map/all_gather | solution.py:38
  107.2 2.4 %fusion = f32[]{:T(128)} fusion(bf16[1,512,1024]{2,1,0:T(8,128)(2,1)} %all-gather.2.cloned.1.call-done), kind=kLoop, calls=%fused_computation.2 | loop fusion | flops 1572863 | bytes 1048580 | tf_op jit(solution)/shard_map/reduce_sum | solution.py:40
  110.3 2.3 %fusion.8 = f32[512,512]{1,0:T(8,128)S(1)} fusion(bf16[1,512,1024]{2,1,0:T(8,128)(2,1)} %all-gather.2.cloned.1.call-done, f32[]{:T(128)S(6)} %add.35), kind=kOutput, calls=%fused_computation.36 | convolution fusion | flops 538443776 | bytes 2097156 | tf_op jit(solution)/shard_map/dot_general | solution.py:43
  112.6 0.0 copy-start
  112.6 1.9 %fusion.4 = f32[512,512]{1,0:T(8,128)S(1)} fusion(f32[512,512]{1,0:T(8,128)S(1)} %fusion.8), kind=kOutput, calls=%fused_computation.11 | convolution fusion | flops 1611399168 | bytes 2097152 | tf_op jit(solution)/shard_map/dot_general | solution.py:20
  114.5 0.0 copy-done
  114.5 1.9 %add_convert_fusion.1 = bf16[512,1024]{1,0:T(8,128)(2,1)S(1)} fusion(f32[512,512]{1,0:T(8,128)S(1)} %fusion.4, f32[]{:T(128)S(6)} %add.35, bf16[1,512,1024]{2,1,0:T(8,128)(2,1)S(1)} %copy-done), kind=kOutput, calls=%fused_computation.5 | convolution fusion | flops 3226468352 | bytes 3145732 | tf_op jit(solution)/shard_map/dot_general | solution.py:22
  116.5 0.7 fusion.11
  117.2 1.9 %fusion.3 = f32[512,512]{1,0:T(8,128)S(1)} fusion(f32[512,512]{1,0:T(8,128)S(1)} %fusion.11), kind=kOutput, calls=%fused_computation.9 | convolution fusion | flops 1611399168 | bytes 2097152 | tf_op jit(solution)/shard_map/dot_general | solution.py:20
  119.1 1.9 %add_convert_fusion = bf16[512,1024]{1,0:T(8,128)(2,1)S(1)} fusion(bf16[512,1024]{1,0:T(8,128)(2,1)S(1)} %add_convert_fusion.1, f32[512,512]{1,0:T(8,128)S(1)} %fusion.3), kind=kOutput, calls=%fused_computation.4 | convolution fusion | flops 3223322624 | bytes 3145728 | tf_op jit(solution)/shard_map/dot_general | solution.py:22
  121.0 0.7 fusion.12
  121.8 1.9 %fusion.2 = f32[512,512]{1,0:T(8,128)S(1)} fusion(f32[512,512]{1,0:T(8,128)S(1)} %fusion.12), kind=kOutput, calls=%fused_computation.7 | convolution fusion | flops 1611399168 | bytes 2097152 | tf_op jit(solution)/shard_map/dot_general | solution.py:20
  123.7 2.0 %fusion.13 = f32[512,1024]{1,0:T(8,128)S(1)} fusion(f32[512,512]{1,0:T(8,128)S(1)} %fusion.2, bf16[512,1024]{1,0:T(8,128)(2,1)S(1)} %add_convert_fusion), kind=kOutput, calls=%fused_computation.39 | convolution fusion | flops 3221225472 | bytes 4194304 | tf_op jit(solution)/shard_map/dot_general | solution.py:22
  125.7 0.0 copy-start.2
  125.7 0.4 copy.7
  126.1 0.5 broadcast.39
  126.7 2.3 %reduce.1 = bf16[1024,8]{1,0:T(8,128)(2,1)S(1)} reduce(bf16[1024,1,8]{2,1,0:T(2,128)(2,1)S(1)} %bitcast.67, bf16[]{:T(256)} %broadcast.39), dimensions={1}, to_apply=%bitcast.48.reduce_sub_computation | reduce | bytes 32770
  128.9 0.3 reshape.27
  129.2 12.9 %all_to_all.15 = bf16[8,2,512]{2,1,0:T(2,128)(2,1)S(1)} all-to-all(bf16[8,2,512]{2,1,0:T(2,128)(2,1)S(1)} %reshape.27), channel_id=1, replica_groups=mesh['shard'=64,'tensor'=8] {'tensor'}, dimensions={0} | all-to-all | bytes 32768 | tf_op jit(solution)/shard_map/all_to_all | solution.py:47
  142.1 0.7 reshape.28
  142.8 0.7 convert_multiply_fusion.1
  143.5 0.2 copy.8
  143.7 0.0 copy-done.2
  143.7 0.0 copy-start.1
  143.7 0.6 multiply_subtract_fusion
  144.3 0.0 copy-done.1
  (9 shorter events, 0.1 us)
Async XLA Ops:
  7.2 100.1 %all-gather.2.cloned.1.call-start = ((), (), s32[]{:S(2)}) async-start(), calls=%async_computation.2 | async-start | bytes 1064960 | tf_op jit(solution)/shard_map/all_gather | solution.py:38
  112.6 1.9 %copy-start = (bf16[1,512,1024]{2,1,0:T(8,128)(2,1)S(1)}, bf16[1,512,1024]{2,1,0:T(8,128)(2,1)}, u32[]{:S(2)}) copy-start(bf16[1,512,1024]{2,1,0:T(8,128)(2,1)} %all-gather.2.cloned.1.call-done) | copy-start | bytes 3145732
  125.7 18.0 %copy-start.2 = (f32[8,8,128]{2,1,0:T(8,128)S(1)}, f32[8,8,128]{2,1,0:T(8,128)}, u32[]{:S(2)}) copy-start(f32[8,8,128]{2,1,0:T(8,128)} %param.5) | copy-start | bytes 98308
  143.7 0.6 copy-start.1
Sparse Core Ops, SparseCore 0:
  23.0 84.2 all-gather.1
